TPU v7x, 32 devices: a whole 2x2x4 slice. The times are simulated.
32 devices in a mesh: ctx: 16 (over z, y, x), tp: 2 (over core).
Axes of the slice: x: 2, y: 2, z: 4, core: 2. Of those that a mesh axis runs over, the one named last changes fastest.
Arguments:
- tokens: bfloat16 [4096, 2688], P(('ctx', 'tp')), may hold values from -6 to 6
- result_grad: bfloat16 [4096, 2688], P(('ctx', 'tp')), may hold values from -6 to 6
- query_weight: bfloat16 [2688, 512], P(None, 'tp'), may hold values from -0.125 to 0.125
- key_weight: bfloat16 [2688, 256], P(None, 'tp'), may hold values from -0.125 to 0.125
- value_weight: bfloat16 [2688, 256], P(None, 'tp'), may hold values from -0.125 to 0.125
- output_weight: bfloat16 [512, 2688], P('tp'), may hold values from -0.5 to 0.5
- query_gain: float32 [128], replicated, may hold values from 0.5 to 1.5
- key_gain: float32 [128], replicated, may hold values from 0.5 to 1.5
Outputs:
- layer_output: bfloat16 [4096, 2688], P(('ctx', 'tp'))
- tokens_grad: bfloat16 [4096, 2688], P(('ctx', 'tp'))
All inputs are finite; a program needn't handle non-finite values.
Results may differ from a plain program's by a relative error of at most 0.012.
Values may be sent and summed in bfloat16 or wider, within the bound.
A program may use at most 64 MiB of HBM per device.

v0:
```python
import jax
import jax.numpy as jnp
from jax import lax
from jax.sharding import PartitionSpec as P

WINDOW = 1024
norm_epsilon = 1e-06
score_scale = 168.0 ** (-0.5)
rope_theta = 10000.0


def from_behind(block, axis, distance):
    devices = range(lax.axis_size(axis))
    route = [(i - distance, i) for i in devices if i - distance in devices]
    return lax.ppermute(block, axis, route)


def rope_tables(positions, head_size):
    half_size = head_size // 2
    exponent = jnp.arange(half_size, dtype=jnp.float32) * (2.0 / head_size)
    frequency = jnp.power(jnp.float32(rope_theta), -exponent)
    angles = positions.astype(jnp.float32)[:, None] * frequency[None, :]
    return (jnp.cos(angles), jnp.sin(angles))


def norm_rope(raw_proj, scale_gain, cosines, sines):
    row_count = raw_proj.shape[0]
    head_size = scale_gain.shape[0]
    split_heads = raw_proj.reshape(row_count, -1, head_size)
    mean_square = jnp.mean(split_heads * split_heads, axis=-1, keepdims=True)
    normed = split_heads * lax.rsqrt(mean_square + norm_epsilon) * scale_gain
    half_size = head_size // 2
    low_half = normed[..., :half_size]
    high_half = normed[..., half_size:]
    cosine_b = cosines[:, None, :]
    sine_b = sines[:, None, :]
    return jnp.concatenate(
        [low_half * cosine_b - high_half * sine_b, high_half * cosine_b + low_half * sine_b],
        axis=-1,
    )


def attend(queries, keys_all, values_all, out_grad, query_first, key_first):
    query_count = queries.shape[0]
    key_count = keys_all.shape[0]
    scores = (
        jnp.einsum("qkgh,ckh->kgqc", queries, keys_all, preferred_element_type=jnp.float32)
        * score_scale
    )
    query_pos = query_first + jnp.arange(query_count, dtype=jnp.int32)
    key_pos = key_first + jnp.arange(key_count, dtype=jnp.int32)
    distance = query_pos[:, None] - key_pos[None, :]
    allowed = (distance >= 0) & (distance < WINDOW) & (key_pos[None, :] >= 0)
    weights_raw = jnp.where(allowed, jnp.exp(scores), jnp.float32(0.0))
    denominator = jnp.sum(weights_raw, axis=-1, keepdims=True)
    weights_soft = weights_raw / denominator
    weights_low = weights_soft.astype(jnp.bfloat16)
    attended_wide = jnp.einsum(
        "kgqc,ckh->qkgh", weights_low, values_all, preferred_element_type=jnp.float32
    )
    attended = lax.optimization_barrier(attended_wide.astype(jnp.bfloat16))
    row_dots = jnp.sum(out_grad.astype(jnp.float32) * attended.astype(jnp.float32), axis=-1)
    prob_grad = jnp.einsum(
        "qkgh,ckh->kgqc", out_grad, values_all, preferred_element_type=jnp.float32
    )
    centered = prob_grad - jnp.transpose(row_dots, (1, 2, 0))[..., None]
    score_grad = (weights_soft * centered * score_scale).astype(jnp.bfloat16)
    query_grad = jnp.einsum(
        "kgqc,ckh->qkgh", score_grad, keys_all, preferred_element_type=jnp.float32
    )
    key_grad = jnp.einsum("kgqc,qkgh->ckh", score_grad, queries, preferred_element_type=jnp.float32)
    value_grad = jnp.einsum(
        "kgqc,qkgh->ckh", weights_low, out_grad, preferred_element_type=jnp.float32
    )
    return (attended, query_grad, key_grad, value_grad)


def on_device(
    tokens, result_grad, query_weight, key_weight, value_weight, output_weight, query_gain, key_gain
):
    local_rows = tokens.shape[0]
    row_count = local_rows * lax.axis_size("tp")
    head_size = query_gain.shape[0]
    query_cols = query_weight.shape[1]
    kv_cols = key_weight.shape[1]
    kv_count = kv_cols // head_size
    per_kv = query_cols // kv_cols
    stacked = jnp.stack([tokens, result_grad])
    portion = lax.all_gather(stacked, "tp", axis=1, tiled=True)
    inputs_part = portion[0]
    gradients_part = portion[1]
    query_rows = jnp.dot(inputs_part, query_weight, preferred_element_type=jnp.float32)
    key_rows = jnp.dot(inputs_part, key_weight, preferred_element_type=jnp.float32)
    value_rows = jnp.dot(inputs_part, value_weight, preferred_element_type=jnp.float32)
    grad_rows = jnp.einsum(
        "nd,hd->nh", gradients_part, output_weight, preferred_element_type=jnp.float32
    )
    joined = jnp.concatenate([query_rows, key_rows, value_rows, grad_rows], axis=1)
    query_raw = joined[:, :query_cols]
    key_raw = joined[:, query_cols : query_cols + kv_cols]
    value_raw = joined[:, query_cols + kv_cols : query_cols + 2 * kv_cols]
    out_grad = (
        joined[:, query_cols + 2 * kv_cols :]
        .astype(jnp.bfloat16)
        .reshape(row_count, kv_count, per_kv, head_size)
    )
    row_first = lax.axis_index("ctx") * row_count
    positions = row_first + jnp.arange(row_count, dtype=jnp.int32)
    cosines, sines = rope_tables(positions, head_size)
    queries = (
        norm_rope(query_raw, query_gain, cosines, sines)
        .astype(jnp.bfloat16)
        .reshape(row_count, kv_count, per_kv, head_size)
    )
    keys_own = norm_rope(key_raw, key_gain, cosines, sines).astype(jnp.bfloat16)
    values_own = value_raw.astype(jnp.bfloat16).reshape(row_count, kv_count, head_size)
    tail_rows = min(row_count, WINDOW)
    reach = WINDOW // tail_rows
    own_tail = jnp.stack([keys_own, values_own])
    arrivals = []
    message = own_tail
    for stride in range(1, reach + 1):
        sender = own_tail
        distance = stride
        message = from_behind(sender, "ctx", distance)
        arrivals.append(message)
    halo_rows = jnp.concatenate(arrivals[::-1], axis=1)
    keys_all = jnp.concatenate([halo_rows[0], keys_own], axis=0)
    values_all = jnp.concatenate([halo_rows[1], values_own], axis=0)
    attended, query_grad, key_grad, value_grad = attend(
        queries, keys_all, values_all, out_grad, row_first, row_first - WINDOW
    )
    attended_flat = attended.reshape(row_count, query_cols)
    halo_grad = jnp.stack([key_grad[:WINDOW], value_grad[:WINDOW]])
    returned = jnp.zeros((2, tail_rows, kv_count, head_size), jnp.float32)
    for turn_index in range(reach):
        portion_stride = turn_index + 1
        sender = halo_grad[
            :, WINDOW - portion_stride * tail_rows : WINDOW - (portion_stride - 1) * tail_rows
        ]
        distance = -(turn_index + 1)
        arrived = from_behind(sender.astype(jnp.bfloat16), "ctx", distance).astype(sender.dtype)
        returned = returned + arrived
    keep_rows = row_count - tail_rows
    key_grad_own = key_grad[WINDOW:]
    value_grad_own = value_grad[WINDOW:]
    key_grad_own = jnp.concatenate([key_grad_own[:keep_rows], key_grad_own + returned[0]], axis=0)
    value_grad_own = jnp.concatenate(
        [value_grad_own[:keep_rows], value_grad_own + returned[1]], axis=0
    )

    def query_shape(raw_proj):
        return norm_rope(raw_proj, query_gain, cosines, sines)

    def key_shape(raw_proj):
        return norm_rope(raw_proj, key_gain, cosines, sines)

    query_back = jax.vjp(query_shape, query_raw)[1](query_grad.reshape(row_count, -1, head_size))[
        0
    ].astype(jnp.bfloat16)
    key_back = jax.vjp(key_shape, key_raw)[1](key_grad_own)[0].astype(jnp.bfloat16)
    value_back = value_grad_own.reshape(row_count, kv_cols).astype(jnp.bfloat16)
    out_part = jnp.dot(attended_flat, output_weight, preferred_element_type=jnp.float32)
    query_rows = query_back
    key_rows = key_back
    value_rows = value_back
    summed = jnp.einsum("nh,dh->nd", query_rows, query_weight, preferred_element_type=jnp.float32)
    summed = summed + jnp.einsum(
        "nh,dh->nd", key_rows, key_weight, preferred_element_type=jnp.float32
    )
    summed = summed + jnp.einsum(
        "nh,dh->nd", value_rows, value_weight, preferred_element_type=jnp.float32
    )
    out_sum, grad_sum = (
        lax.psum_scatter(
            out_part.astype(jnp.bfloat16), "tp", scatter_dimension=0, tiled=True
        ).astype(jnp.float32),
        lax.psum_scatter(summed.astype(jnp.bfloat16), "tp", scatter_dimension=0, tiled=True).astype(
            jnp.float32
        ),
    )
    layer_output = (tokens.astype(jnp.float32) + out_sum).astype(jnp.bfloat16)
    tokens_grad = (result_grad.astype(jnp.float32) + grad_sum).astype(jnp.bfloat16)
    return (layer_output, tokens_grad)


def solution(mesh):
    in_specs = (
        P(("ctx", "tp"), None),
        P(("ctx", "tp"), None),
        P(None, "tp"),
        P(None, "tp"),
        P(None, "tp"),
        P("tp", None),
        P(),
        P(),
    )
    out_specs = (P(("ctx", "tp"), None), P(("ctx", "tp"), None))
    return jax.shard_map(
        on_device, mesh=mesh, in_specs=in_specs, out_specs=out_specs, check_vma=False
    )
```

profile of v0, /device:TPU:0, one launch (start us, length us, event | category | flops | bytes accessed | tf_op | source)
XLA Modules:
  0.0 92.2 jit_solution(1839996132509159438)
XLA Ops:
  7.2 2.7 %pad_maximum_fusion = bf16[2,128,2688]{2,1,0:T(8,128)(2,1)} fusion(bf16[1,128,2688]{2,1,0:T(8,128)(2,1)} %bitcast.158, bf16[1,128,2688]{2,1,0:T(8,128)(2,1)} %bitcast.157), kind=kLoop, calls=%fused_computation.20 | loop fusion | flops 688128 | bytes 2752512 | tf_op jit(solution)/shard_map/stack | solution.py:88
  10.0 1.3 %copy-done.1 = bf16[2688,256]{1,0:T(8,128)(2,1)S(1)} copy-done((bf16[2688,256]{1,0:T(8,128)(2,1)S(1)}, bf16[2688,256]{1,0:T(8,128)(2,1)}, u32[]{:S(2)}) %copy-start.1) | copy-done | bytes 1376280
  11.2 1.7 %copy.30 = bf16[256,2688]{1,0:T(8,128)(2,1)} copy(bf16[256,2688]{0,1:T(8,128)(2,1)S(1)} %bitcast.156) | data formatting | bytes 2752512 | tf_op jit(solution)/shard_map/dot_general | solution.py:92
  13.0 0.3 multiply_cosine_fusion
  13.3 1.6 %fusion.20 = pred[256,1280]{0,1:T(8,128)(4,1)} fusion(s32[1280]{0:T(1024)S(1)} %iota_add_fusion, s32[256]{0:T(256)S(1)} %iota_add_fusion.1, pred[1280]{0:T(1024)(128)(4,1)S(1)} %broadcast_compare_fusion), kind=kLoop, calls=%fused_computation.34 | loop fusion | flops 1638400 | bytes 335104 | tf_op jit(solution)/shard_map/and | solution.py:53
  14.9 9.5 %all-gather.2.cloned.1.call-done = bf16[2,256,2688]{2,1,0:T(8,128)(2,1)} async-done(((bf16[2,128,2688]{2,1,0:T(8,128)(2,1)}), bf16[2,256,2688]{2,1,0:T(8,128)(2,1)}) %all-gather.2.cloned.1.call-update) | async-done | bytes 2752528 | tf_op jit(solution)/shard_map/all_gather | solution.py:89
  24.3 2.3 %multiply_reduce_fusion.2 = (f32[256]{0:T(256)S(1)}, f32[256,128]{0,1:T(8,128)S(1)}) fusion(bf16[2688,128]{1,0:T(8,128)(2,1)} %param.11, bf16[2,256,2688]{2,1,0:T(8,128)(2,1)} %all-gather.2.cloned.1.call-done), kind=kOutput, calls=%fused_computation.77 | convolution fusion | flops 176226048 | bytes 2196480 | tf_op jit(solution)/shard_map/dot_general | solution.py:93
  26.6 0.1 multiply_bitcast_fusion
  26.8 0.3 fusion.51
  27.1 2.0 %fusion.28 = bf16[256,128]{0,1:T(8,128)(2,1)S(1)} fusion(bf16[2688,128]{1,0:T(8,128)(2,1)S(1)} %copy-done.8, bf16[2,256,2688]{2,1,0:T(8,128)(2,1)} %all-gather.2.cloned.1.call-done), kind=kOutput, calls=%fused_computation.39 | convolution fusion | flops 176193536 | bytes 2129920 | tf_op jit(solution)/shard_map/dot_general | solution.py:94
  29.1 3.6 %collective-permute-start.3 = (bf16[2,256,1,128]{1,3,2,0:T(8,128)(2,1)S(1)}, bf16[2,256,1,128]{1,3,2,0:T(8,128)(2,1)S(1)}, u32[]{:S(2)}, u32[]{:S(2)}) collective-permute-start(bf16[2,256,1,128]{1,3,2,0:T(8,128)(2,1)S(1)} %pad_maximum_fusion.1), channel_id=1, source_target_pairs={{0,2},{2,4},{4,6},{6,8},{8,10},{10,12},{12,14},{14,16},{16,18},{18... | collective-permute-start | bytes 393224 | tf_op jit(solution)/shard_map/ppermute | solution.py:15
  32.8 3.4 %collective-permute-start.2 = (bf16[2,256,1,128]{1,3,2,0:T(8,128)(2,1)S(1)}, bf16[2,256,1,128]{1,3,2,0:T(8,128)(2,1)S(1)}, u32[]{:S(2)}, u32[]{:S(2)}) collective-permute-start(bf16[2,256,1,128]{1,3,2,0:T(8,128)(2,1)S(1)} %pad_maximum_fusion.1), channel_id=1, source_target_pairs={{0,4},{2,6},{4,8},{6,10},{8,12},{10,14},{12,16},{14,18},{16,20},{1... | collective-permute-start | bytes 393224 | tf_op jit(solution)/shard_map/ppermute | solution.py:15
  36.2 4.3 %collective-permute-start.1 = (bf16[2,256,1,128]{1,3,2,0:T(8,128)(2,1)S(1)}, bf16[2,256,1,128]{1,3,2,0:T(8,128)(2,1)S(1)}, u32[]{:S(2)}, u32[]{:S(2)}) collective-permute-start(bf16[2,256,1,128]{1,3,2,0:T(8,128)(2,1)S(1)} %pad_maximum_fusion.1), channel_id=1, source_target_pairs={{0,6},{2,8},{4,10},{6,12},{8,14},{10,16},{12,18},{14,20},{16,22},{... | collective-permute-start | bytes 393224 | tf_op jit(solution)/shard_map/ppermute | solution.py:15
  40.5 3.4 %collective-permute-start = (bf16[2,256,1,128]{1,3,2,0:T(8,128)(2,1)S(1)}, bf16[2,256,1,128]{1,3,2,0:T(8,128)(2,1)S(1)}, u32[]{:S(2)}, u32[]{:S(2)}) collective-permute-start(bf16[2,256,1,128]{1,3,2,0:T(8,128)(2,1)S(1)} %pad_maximum_fusion.1), channel_id=1, source_target_pairs={{0,8},{2,10},{4,12},{6,14},{8,16},{10,18},{12,20},{14,22},{16,24},... | collective-permute-start | bytes 393224 | tf_op jit(solution)/shard_map/ppermute | solution.py:15
  43.9 0.6 multiply_reduce_fusion.1
  44.6 0.1 multiply_multiply_fusion
  44.7 0.6 fusion.21
  45.3 1.1 %collective-permute-done = bf16[2,256,1,128]{1,3,2,0:T(8,128)(2,1)S(1)} collective-permute-done((bf16[2,256,1,128]{1,3,2,0:T(8,128)(2,1)S(1)}, bf16[2,256,1,128]{1,3,2,0:T(8,128)(2,1)S(1)}, u32[]{:S(2)}, u32[]{:S(2)}) %collective-permute-start) | collective-permute-done | bytes 131104 | tf_op jit(solution)/shard_map/ppermute | solution.py:15
  46.5 0.8 fusion.73
  47.3 0.3 fusion.31
  47.6 0.5 convolution_bitcast_fusion.1
  48.1 0.3 fusion.25
  48.5 0.6 fusion.8
  49.1 0.3 convolution_bitcast_fusion.3
  49.5 0.6 convolution_bitcast_fusion.2
  50.0 0.1 slice_bitcast_fusion.4
  50.2 0.8 fusion.72
  51.0 1.7 %convolution_convert_fusion = bf16[256,2688]{1,0:T(8,128)(2,1)} fusion(bf16[256,256]{0,1:T(8,128)(2,1)S(1)} %bitcast.160, bf16[256,2688]{1,0:T(8,128)(2,1)S(1)} %copy-done), kind=kOutput, calls=%fused_computation.3 | convolution fusion | flops 353009664 | bytes 2883584 | tf_op jit(solution)/shard_map/dot_general | solution.py:163
  52.8 1.3 %collective-permute-start.4 = (bf16[2,256,1,128]{1,3,2,0:T(8,128)(2,1)}, bf16[2,256,1,128]{1,3,2,0:T(8,128)(2,1)S(1)}, u32[]{:S(2)}, u32[]{:S(2)}) collective-permute-start(bf16[2,256,1,128]{1,3,2,0:T(8,128)(2,1)} %get-tuple-element.2), channel_id=1, source_target_pairs={{2,0},{4,2},{6,4},{8,6},{10,8},{12,10},{14,12},{16,14},{18,16},{20... | collective-permute-start | bytes 393224 | tf_op jit(solution)/shard_map/ppermute | solution.py:15
  54.1 1.3 %collective-permute-start.7 = (bf16[2,256,1,128]{1,3,2,0:T(8,128)(2,1)}, bf16[2,256,1,128]{1,3,2,0:T(8,128)(2,1)S(1)}, u32[]{:S(2)}, u32[]{:S(2)}) collective-permute-start(bf16[2,256,1,128]{1,3,2,0:T(8,128)(2,1)} %get-tuple-element.3), channel_id=1, source_target_pairs={{8,0},{10,2},{12,4},{14,6},{16,8},{18,10},{20,12},{22,14},{24,16},... | collective-permute-start | bytes 393224 | tf_op jit(solution)/shard_map/ppermute | solution.py:15
  55.4 1.3 %collective-permute-start.6 = (bf16[2,256,1,128]{1,3,2,0:T(8,128)(2,1)}, bf16[2,256,1,128]{1,3,2,0:T(8,128)(2,1)S(1)}, u32[]{:S(2)}, u32[]{:S(2)}) collective-permute-start(bf16[2,256,1,128]{1,3,2,0:T(8,128)(2,1)} %get-tuple-element.4), channel_id=1, source_target_pairs={{6,0},{8,2},{10,4},{12,6},{14,8},{16,10},{18,12},{20,14},{22,16},{... | collective-permute-start | bytes 393224 | tf_op jit(solution)/shard_map/ppermute | solution.py:15
  56.7 1.3 %collective-permute-start.5 = (bf16[2,256,1,128]{1,3,2,0:T(8,128)(2,1)}, bf16[2,256,1,128]{1,3,2,0:T(8,128)(2,1)S(1)}, u32[]{:S(2)}, u32[]{:S(2)}) collective-permute-start(bf16[2,256,1,128]{1,3,2,0:T(8,128)(2,1)} %get-tuple-element.5), channel_id=1, source_target_pairs={{4,0},{6,2},{8,4},{10,6},{12,8},{14,10},{16,12},{18,14},{20,16},{2... | collective-permute-start | bytes 393224 | tf_op jit(solution)/shard_map/ppermute | solution.py:15
  58.0 0.8 multiply_reduce_fusion
  58.8 0.8 fusion.35
  59.6 0.6 fusion.74
  60.2 4.8 %collective-permute-done.7 = bf16[2,256,1,128]{1,3,2,0:T(8,128)(2,1)S(1)} collective-permute-done((bf16[2,256,1,128]{1,3,2,0:T(8,128)(2,1)}, bf16[2,256,1,128]{1,3,2,0:T(8,128)(2,1)S(1)}, u32[]{:S(2)}, u32[]{:S(2)}) %collective-permute-start.7) | collective-permute-done | bytes 131104 | tf_op jit(solution)/shard_map/ppermute | solution.py:15
  65.0 1.3 %collective-permute-done.5 = bf16[2,256,1,128]{1,3,2,0:T(8,128)(2,1)S(1)} collective-permute-done((bf16[2,256,1,128]{1,3,2,0:T(8,128)(2,1)}, bf16[2,256,1,128]{1,3,2,0:T(8,128)(2,1)S(1)}, u32[]{:S(2)}, u32[]{:S(2)}) %collective-permute-start.5) | collective-permute-done | bytes 131104 | tf_op jit(solution)/shard_map/ppermute | solution.py:15
  66.3 0.1 convert_add_fusion
  66.4 0.9 %fusion.40 = f32[256,1,128]{0,2,1:T(8,128)S(1)} fusion(f32[2,256,1,128]{1,3,2,0:T(8,128)S(1)} %convert_add_fusion, f32[1280,1,128]{0,2,1:T(8,128)} %copy-done.5), kind=kLoop, calls=%fused_computation.66 | loop fusion | flops 32768 | bytes 393216 | tf_op jit(solution)/shard_map/add | solution.py:147
  67.3 0.3 fusion.54
  67.7 0.1 fusion.41
  67.8 0.6 convolution_add_fusion.1
  68.5 0.5 copy-done.9
  68.9 2.5 %fusion = bf16[256,2688]{1,0:T(8,128)(2,1)} fusion(f32[256,2688]{1,0:T(8,128)S(1)} %convolution_add_fusion.1, bf16[2688,128]{1,0:T(8,128)(2,1)S(1)} %copy-done.9, f32[2,256,1,128]{1,3,2,0:T(8,128)S(1)} %convert_add_fusion, f32[1280,1,128]{0,2,1:T(8,128)} %copy-done.4), kind=kOutput, calls=%fused_computation.2 | convolution fusion | flops 177602560 | bytes 5079040 | tf_op jit(solution)/shard_map/nh,dh->nd/dot_general | solution.py:171
  71.5 1.0 %copy-done.2 = bf16[128,2688]{1,0:T(8,128)(2,1)S(1)} copy-done((bf16[128,2688]{1,0:T(8,128)(2,1)S(1)}, bf16[128,2688]{1,0:T(8,128)(2,1)}, u32[]{:S(2)}) %copy-start.2) | copy-done | bytes 688152
  72.6 2.1 %add_convert_fusion.1 = bf16[128,2688]{1,0:T(8,128)(2,1)} fusion(bf16[128,2688]{1,0:T(8,128)(2,1)} %reduce-scatter.3.cloned.1.call-done, bf16[128,2688]{1,0:T(8,128)(2,1)S(1)} %copy-done.2), kind=kLoop, calls=%fused_computation.28 | loop fusion | flops 1376256 | bytes 2064384 | tf_op jit(solution)/shard_map/convert_element_type | solution.py:182
  74.7 8.9 %reduce-scatter.5.cloned.1.call-done = bf16[128,2688]{1,0:T(8,128)(2,1)} async-done(((bf16[256,2688]{1,0:T(8,128)(2,1)}), bf16[128,2688]{1,0:T(8,128)(2,1)}) %reduce-scatter.5.cloned.1.call-update) | async-done | bytes 688144 | tf_op jit(solution)/shard_map/reduce_scatter | solution.py:178
  83.6 2.1 %add_convert_fusion = bf16[128,2688]{1,0:T(8,128)(2,1)} fusion(bf16[128,2688]{1,0:T(8,128)(2,1)} %reduce-scatter.5.cloned.1.call-done, bf16[128,2688]{1,0:T(8,128)(2,1)S(1)} %copy-done.3), kind=kLoop, calls=%fused_computation.27 | loop fusion | flops 1376256 | bytes 2064384 | tf_op jit(solution)/shard_map/convert_element_type | solution.py:183
  (66 shorter events, 0.7 us)
Async XLA Ops:
  7.2 37.5 %copy-start = (bf16[256,2688]{1,0:T(8,128)(2,1)S(1)}, bf16[256,2688]{1,0:T(8,128)(2,1)}, u32[]{:S(2)}) copy-start(bf16[256,2688]{1,0:T(8,128)(2,1)} %param.13) | copy-start | bytes 4128772
  7.2 17.1 %all-gather.2.cloned.1.call-start = ((), (), s32[]{:S(2)}) async-start(), calls=%async_computation.2 | async-start | bytes 4128768 | tf_op jit(solution)/shard_map/all_gather | solution.py:89
  9.9 1.3 %copy-start.1 = (bf16[2688,256]{1,0:T(8,128)(2,1)S(1)}, bf16[2688,256]{1,0:T(8,128)(2,1)}, u32[]{:S(2)}) copy-start(bf16[2688,256]{1,0:T(8,128)(2,1)} %param.10) | copy-start | bytes 4128772
  9.9 61.6 %reduce-scatter.3.cloned.1.call-start = ((), (), s32[]{:S(2)}) async-start(), calls=%async_computation.3 | async-start | bytes 2064384 | tf_op jit(solution)/shard_map/reduce_scatter | solution.py:175
  12.9 13.9 %copy-start.13 = (f32[64]{0:T(128)}, f32[64]{0:T(128)S(1)}, u32[]{:S(2)}) copy-start(f32[64]{0:T(128)S(1)} %negate_power_fusion) | copy-start | bytes 772
  12.9 13.7 %copy-start.11 = (f32[128]{0:T(128)S(1)}, f32[128]{0:T(128)}, u32[]{:S(2)}) copy-start(f32[128]{0:T(128)} %param.15) | copy-start | bytes 1540
  24.3 2.8 %copy-start.8 = (bf16[2688,128]{1,0:T(8,128)(2,1)S(1)}, bf16[2688,128]{1,0:T(8,128)(2,1)}, u32[]{:S(2)}) copy-start(bf16[2688,128]{1,0:T(8,128)(2,1)} %param.12) | copy-start | bytes 2064388
  24.3 19.6 %copy-start.18 = (bf16[2,256,2688]{2,1,0:T(8,128)(2,1)S(1)}, bf16[2,256,2688]{2,1,0:T(8,128)(2,1)}, u32[]{:S(2)}) copy-start(bf16[2,256,2688]{2,1,0:T(8,128)(2,1)} %all-gather.2.cloned.1.call-done) | copy-start | bytes 8257540
  26.6 2.5 %copy-start.16 = (f32[256]{0:T(256)}, f32[256]{0:T(256)S(1)}, u32[]{:S(2)}) copy-start(f32[256]{0:T(256)S(1)} %get-tuple-element.18) | copy-start | bytes 3076
  26.7 17.1 %copy-start.6 = (bf16[256,2688]{1,0:T(8,128)(2,1)S(1)}, bf16[256,2688]{1,0:T(8,128)(2,1)}, u32[]{:S(2)}) copy-start(bf16[256,2688]{1,0:T(8,128)(2,1)} %copy.30) | copy-start | bytes 4128772
  29.1 17.3 %collective-permute-start.3 = (bf16[2,256,1,128]{1,3,2,0:T(8,128)(2,1)S(1)}, bf16[2,256,1,128]{1,3,2,0:T(8,128)(2,1)S(1)}, u32[]{:S(2)}, u32[]{:S(2)}) collective-permute-start(bf16[2,256,1,128]{1,3,2,0:T(8,128)(2,1)S(1)} %pad_maximum_fusion.1), channel_id=1, source_target_pairs={{0,2},{2,4},{4,6},{6,8},{8,10},{10,12},{12,14},{14,16},{16,18},{18... | collective-permute-start | bytes 393224 | tf_op jit(solution)/shard_map/ppermute | solution.py:15
  32.8 13.6 %collective-permute-start.2 = (bf16[2,256,1,128]{1,3,2,0:T(8,128)(2,1)S(1)}, bf16[2,256,1,128]{1,3,2,0:T(8,128)(2,1)S(1)}, u32[]{:S(2)}, u32[]{:S(2)}) collective-permute-start(bf16[2,256,1,128]{1,3,2,0:T(8,128)(2,1)S(1)} %pad_maximum_fusion.1), channel_id=1, source_target_pairs={{0,4},{2,6},{4,8},{6,10},{8,12},{10,14},{12,16},{14,18},{16,20},{1... | collective-permute-start | bytes 393224 | tf_op jit(solution)/shard_map/ppermute | solution.py:15
  36.2 10.2 %collective-permute-start.1 = (bf16[2,256,1,128]{1,3,2,0:T(8,128)(2,1)S(1)}, bf16[2,256,1,128]{1,3,2,0:T(8,128)(2,1)S(1)}, u32[]{:S(2)}, u32[]{:S(2)}) collective-permute-start(bf16[2,256,1,128]{1,3,2,0:T(8,128)(2,1)S(1)} %pad_maximum_fusion.1), channel_id=1, source_target_pairs={{0,6},{2,8},{4,10},{6,12},{8,14},{10,16},{12,18},{14,20},{16,22},{... | collective-permute-start | bytes 393224 | tf_op jit(solution)/shard_map/ppermute | solution.py:15
  40.5 5.9 %collective-permute-start = (bf16[2,256,1,128]{1,3,2,0:T(8,128)(2,1)S(1)}, bf16[2,256,1,128]{1,3,2,0:T(8,128)(2,1)S(1)}, u32[]{:S(2)}, u32[]{:S(2)}) collective-permute-start(bf16[2,256,1,128]{1,3,2,0:T(8,128)(2,1)S(1)} %pad_maximum_fusion.1), channel_id=1, source_target_pairs={{0,8},{2,10},{4,12},{6,14},{8,16},{10,18},{12,20},{14,22},{16,24},... | collective-permute-start | bytes 393224 | tf_op jit(solution)/shard_map/ppermute | solution.py:15
  43.9 0.7 copy-start.15
  45.2 1.3 %copy-start.10 = (pred[256,1280]{0,1:T(8,128)(4,1)S(1)}, pred[256,1280]{0,1:T(8,128)(4,1)}, u32[]{:S(2)}) copy-start(pred[256,1280]{0,1:T(8,128)(4,1)} %fusion.20) | copy-start | bytes 983044
  48.1 1.9 %copy-start.4 = (f32[1280,1,128]{0,2,1:T(8,128)}, f32[1280,1,128]{0,2,1:T(8,128)S(1)}, u32[]{:S(2)}) copy-start(f32[1280,1,128]{0,2,1:T(8,128)S(1)} %convolution_bitcast_fusion.1) | copy-start | bytes 1966084
  50.0 1.0 %copy-start.5 = (f32[1280,1,128]{0,2,1:T(8,128)}, f32[1280,1,128]{0,2,1:T(8,128)S(1)}, u32[]{:S(2)}) copy-start(f32[1280,1,128]{0,2,1:T(8,128)S(1)} %convolution_bitcast_fusion.2) | copy-start | bytes 1966084
  52.7 30.9 %reduce-scatter.5.cloned.1.call-start = ((), (), s32[]{:S(2)}) async-start(), calls=%async_computation.4 | async-start | bytes 2064384 | tf_op jit(solution)/shard_map/reduce_scatter | solution.py:178
  52.8 7.4 %collective-permute-start.4 = (bf16[2,256,1,128]{1,3,2,0:T(8,128)(2,1)}, bf16[2,256,1,128]{1,3,2,0:T(8,128)(2,1)S(1)}, u32[]{:S(2)}, u32[]{:S(2)}) collective-permute-start(bf16[2,256,1,128]{1,3,2,0:T(8,128)(2,1)} %get-tuple-element.2), channel_id=1, source_target_pairs={{2,0},{4,2},{6,4},{8,6},{10,8},{12,10},{14,12},{16,14},{18,16},{20... | collective-permute-start | bytes 393224 | tf_op jit(solution)/shard_map/ppermute | solution.py:15
  54.1 10.9 %collective-permute-start.7 = (bf16[2,256,1,128]{1,3,2,0:T(8,128)(2,1)}, bf16[2,256,1,128]{1,3,2,0:T(8,128)(2,1)S(1)}, u32[]{:S(2)}, u32[]{:S(2)}) collective-permute-start(bf16[2,256,1,128]{1,3,2,0:T(8,128)(2,1)} %get-tuple-element.3), channel_id=1, source_target_pairs={{8,0},{10,2},{12,4},{14,6},{16,8},{18,10},{20,12},{22,14},{24,16},... | collective-permute-start | bytes 393224 | tf_op jit(solution)/shard_map/ppermute | solution.py:15
  55.4 9.6 %collective-permute-start.6 = (bf16[2,256,1,128]{1,3,2,0:T(8,128)(2,1)}, bf16[2,256,1,128]{1,3,2,0:T(8,128)(2,1)S(1)}, u32[]{:S(2)}, u32[]{:S(2)}) collective-permute-start(bf16[2,256,1,128]{1,3,2,0:T(8,128)(2,1)} %get-tuple-element.4), channel_id=1, source_target_pairs={{6,0},{8,2},{10,4},{12,6},{14,8},{16,10},{18,12},{20,14},{22,16},{... | collective-permute-start | bytes 393224 | tf_op jit(solution)/shard_map/ppermute | solution.py:15
  56.7 9.6 %collective-permute-start.5 = (bf16[2,256,1,128]{1,3,2,0:T(8,128)(2,1)}, bf16[2,256,1,128]{1,3,2,0:T(8,128)(2,1)S(1)}, u32[]{:S(2)}, u32[]{:S(2)}) collective-permute-start(bf16[2,256,1,128]{1,3,2,0:T(8,128)(2,1)} %get-tuple-element.5), channel_id=1, source_target_pairs={{4,0},{6,2},{8,4},{10,6},{12,8},{14,10},{16,12},{18,14},{20,16},{2... | collective-permute-start | bytes 393224 | tf_op jit(solution)/shard_map/ppermute | solution.py:15
  59.6 7.7 %copy-start.14 = (f32[64]{0:T(128)S(1)}, f32[64]{0:T(128)}, u32[]{:S(2)}) copy-start(f32[64]{0:T(128)} %copy-done.13) | copy-start | bytes 772
  60.2 7.5 %copy-start.12 = (f32[128]{0:T(128)S(1)}, f32[128]{0:T(128)}, u32[]{:S(2)}) copy-start(f32[128]{0:T(128)} %param.15) | copy-start | bytes 1540
  60.2 7.6 %copy-start.17 = (f32[256]{0:T(256)S(1)}, f32[256]{0:T(256)}, u32[]{:S(2)}) copy-start(f32[256]{0:T(256)} %copy-done.16) | copy-start | bytes 3076
  60.2 7.6 %copy-start.7 = (bf16[2688,128]{1,0:T(8,128)(2,1)S(1)}, bf16[2688,128]{1,0:T(8,128)(2,1)}, u32[]{:S(2)}) copy-start(bf16[2688,128]{1,0:T(8,128)(2,1)} %param.11) | copy-start | bytes 2064388
  67.8 1.1 %copy-start.9 = (bf16[2688,128]{1,0:T(8,128)(2,1)S(1)}, bf16[2688,128]{1,0:T(8,128)(2,1)}, u32[]{:S(2)}) copy-start(bf16[2688,128]{1,0:T(8,128)(2,1)} %param.12) | copy-start | bytes 2064388
  71.5 1.1 %copy-start.2 = (bf16[128,2688]{1,0:T(8,128)(2,1)S(1)}, bf16[128,2688]{1,0:T(8,128)(2,1)}, u32[]{:S(2)}) copy-start(bf16[128,2688]{1,0:T(8,128)(2,1)} %param.8) | copy-start | bytes 2064388
  71.5 12.1 %copy-start.3 = (bf16[128,2688]{1,0:T(8,128)(2,1)S(1)}, bf16[128,2688]{1,0:T(8,128)(2,1)}, u32[]{:S(2)}) copy-start(bf16[128,2688]{1,0:T(8,128)(2,1)} %param.9) | copy-start | bytes 2064388
Sparse Core Ops, SparseCore 0:
  10.0 14.2 all-gather.1
  52.8 8.9 reduce-scatter.2
  71.6 11.9 reduce-scatter.4
where the time goes:
time: 92.8 us; the launch traced here: 92.2 us
  waiting for transfers between devices  25.6 us (28%)
  starting transfers between devices  20 us (22%)
  between operations  14.3 us (15%)
  matrix products  14 us (15%)
  other arithmetic  12.8 us (14%)
  local copies, waits for them, and re-layouts  5.53 us (6%)
    ppermute x8, starting transfers between devices, from_behind(): return lax.ppermute(block, axis, route)  19.9 us
    all_gather x1, waiting for transfers between devices, on_device(): portion = lax.all_gather(stacked, 'tp', axis=1, tiled=True)  9.45 us
    reduce_scatter x1, waiting for transfers between devices, on_device(): lax.psum_scatter(summed.astype(jnp.bfloat16), 'tp', scatter_dimension=0,...  8.92 us
    ppermute x8, waiting for transfers between devices, from_behind(): return lax.ppermute(block, axis, route)  7.18 us
    unnamed x41, local copies, waits for them, and re-layouts  2.91 us
    another operation x1, other arithmetic, on_device(): stacked = jnp.stack([tokens, result_grad])  2.66 us
    dot_general x1, matrix products, on_device(): jnp.einsum('nh,dh->nd', value_rows, value_weight, preferred_element_type=...  2.54 us
    dot_general x1, matrix products, on_device(): jnp.dot(inputs_part, key_weight, preferred_element_type=jnp.float32)  2.28 us
  transfers between devices with their start and end apart: 11, of which 5 were waited for; matrix products, arithmetic and copies ran while one was open for 15% of the time, Pallas kernels for 0%

commit v1 on v0

--- a/solution.py
+++ b/solution.py
@@ -86,7 +86,8 @@
     kv_count = kv_cols // head_size
     per_kv = query_cols // kv_cols
     stacked = jnp.stack([tokens, result_grad])
-    portion = lax.all_gather(stacked, "tp", axis=1, tiled=True)
+    parts = lax.all_gather(stacked, "tp", axis=0, tiled=False)
+    portion = jnp.concatenate(parts, axis=1)
     inputs_part = portion[0]
     gradients_part = portion[1]
     query_rows = jnp.dot(inputs_part, query_weight, preferred_element_type=jnp.float32)

time: 92.8 us -> 98.8 us (1.065)
  waiting for transfers between devices: 25.6 us -> 29.1 us
  other arithmetic: 12.8 us -> 16 us
  local copies, waits for them, and re-layouts: 5.53 us -> 7.9 us
  matrix products: 14 us -> 11.7 us
    all_gather x0 -> x1, local copies, waits for them, and re-layouts: none -> 1.99 us  [on_device(): parts = lax.all_gather(stacked, 'tp', axis=0, tiled=False)]
    dot_general x1, matrix products: 2.28 us -> 0.62 us  [on_device(): jnp.dot(inputs_part, key_weight, preferred_element_type=jnp.float32)]
    ppermute x8, waiting for transfers between devices: 7.18 us -> 8.61 us  [from_behind(): return lax.ppermute(block, axis, route)]
    dot_general x1, matrix products: 2.01 us -> 0.61 us  [on_device(): jnp.dot(inputs_part, value_weight, preferred_element_type=jnp.float32)]
    reduce_scatter x1, waiting for transfers between devices: 0.02 us -> 1.38 us  [on_device(): lax.psum_scatter(out_part.astype(jnp.bfloat16), 'tp', scatter_dimension=0...]
    reduce_scatter x1, waiting for transfers between devices: 8.92 us -> 10.2 us  [on_device(): lax.psum_scatter(summed.astype(jnp.bfloat16), 'tp', scatter_dimension=0,...]
    add x1, other arithmetic: 0.07 us -> 1.16 us  [on_device(): returned = returned + arrived]
    unnamed x41 -> x37, local copies, waits for them, and re-layouts: 2.91 us -> 3.08 us
  transfers between devices with their start and end apart: 11 -> 11, of which waited for: 5 -> 7; matrix products, arithmetic and copies ran while one was open for 15% -> 19% of each run, Pallas kernels for 0% -> 0%
where the time goes in v1:
time: 98.8 us; the launch traced here: 98.1 us
  waiting for transfers between devices  29.1 us (29%)
  starting transfers between devices  19.1 us (19%)
  other arithmetic  16 us (16%)
  between operations  14.2 us (14%)
  matrix products  11.7 us (12%)
  local copies, waits for them, and re-layouts  7.9 us (8%)
    ppermute x8, starting transfers between devices, from_behind(): return lax.ppermute(block, axis, route)  19 us
    reduce_scatter x1, waiting for transfers between devices, on_device(): lax.psum_scatter(summed.astype(jnp.bfloat16), 'tp', scatter_dimension=0,...  10.2 us
    all_gather x1, waiting for transfers between devices, on_device(): parts = lax.all_gather(stacked, 'tp', axis=0, tiled=False)  8.87 us
    ppermute x8, waiting for transfers between devices, from_behind(): return lax.ppermute(block, axis, route)  8.61 us
    unnamed x37, local copies, waits for them, and re-layouts  3.08 us
    another operation x1, other arithmetic, on_device(): stacked = jnp.stack([tokens, result_grad])  2.66 us
    dot_general x1, matrix products, on_device(): jnp.einsum('nh,dh->nd', value_rows, value_weight, preferred_element_type=...  2.56 us
    convert_element_type x1, other arithmetic, on_device(): layer_output = (tokens.astype(jnp.float32) + out_sum).astype(jnp.bfloat16)  2.1 us
  transfers between devices with their start and end apart: 11, of which 7 were waited for; matrix products, arithmetic and copies ran while one was open for 19% of the time, Pallas kernels for 0%

profile of v1, /device:TPU:0, one launch (start us, length us, event | category | flops | bytes accessed | tf_op | source)
XLA Modules:
  0.0 98.1 jit_solution(714439358830853837)
XLA Ops:
  7.2 2.7 %pad_maximum_fusion = bf16[2,128,2688]{2,1,0:T(8,128)(2,1)} fusion(bf16[1,128,2688]{2,1,0:T(8,128)(2,1)} %bitcast.156, bf16[1,128,2688]{2,1,0:T(8,128)(2,1)} %bitcast.155), kind=kLoop, calls=%fused_computation.19 | loop fusion | flops 688128 | bytes 2752512 | tf_op jit(solution)/shard_map/stack | solution.py:88
  10.0 1.3 %copy-done.1 = bf16[2688,256]{1,0:T(8,128)(2,1)S(1)} copy-done((bf16[2688,256]{1,0:T(8,128)(2,1)S(1)}, bf16[2688,256]{1,0:T(8,128)(2,1)}, u32[]{:S(2)}) %copy-start.1) | copy-done | bytes 1376280
  11.2 1.7 %copy.42 = bf16[256,2688]{1,0:T(8,128)(2,1)} copy(bf16[256,2688]{0,1:T(8,128)(2,1)S(1)} %bitcast.153) | data formatting | bytes 2752512 | tf_op jit(solution)/shard_map/dot_general | solution.py:93
  12.9 0.9 multiply_cosine_fusion
  13.9 1.6 %fusion.13 = pred[256,1280]{0,1:T(8,128)(4,1)} fusion(s32[1280]{0:T(1024)S(1)} %iota_add_fusion, s32[256]{0:T(256)S(1)} %iota_add_fusion.1, pred[1280]{0:T(1024)(128)(4,1)S(1)} %broadcast_compare_fusion), kind=kLoop, calls=%fused_computation.27 | loop fusion | flops 1638400 | bytes 335104 | tf_op jit(solution)/shard_map/and | solution.py:53
  15.5 8.9 %all-gather.3.cloned.1.call-done = bf16[4,128,2688]{2,1,0:T(8,128)(2,1)} async-done(((bf16[2,128,2688]{2,1,0:T(8,128)(2,1)}), bf16[4,128,2688]{2,1,0:T(8,128)(2,1)}) %all-gather.3.cloned.1.call-update) | async-done | bytes 2752528 | tf_op jit(solution)/shard_map/all_gather | solution.py:89
  24.3 2.0 %copy.45 = bf16[2,2,128,2688]{3,2,0,1:T(8,128)(2,1)S(1)} copy(bf16[2,2,128,2688]{3,2,1,0:T(8,128)(2,1)} %bitcast.154) | data formatting | bytes 5505024 | tf_op jit(solution)/shard_map/all_gather | solution.py:89
  26.6 0.8 copy-done.3
  27.4 0.6 multiply_reduce_fusion.2
  28.1 0.6 copy-done.8
  28.8 0.3 fusion.37
  29.1 0.6 convolution_convert_fusion.2
  29.8 3.7 %collective-permute-start = (bf16[2,256,1,128]{1,3,2,0:T(8,128)(2,1)S(1)}, bf16[2,256,1,128]{1,3,2,0:T(8,128)(2,1)S(1)}, u32[]{:S(2)}, u32[]{:S(2)}) collective-permute-start(bf16[2,256,1,128]{1,3,2,0:T(8,128)(2,1)S(1)} %pad_maximum_fusion.1), channel_id=1, source_target_pairs={{0,8},{2,10},{4,12},{6,14},{8,16},{10,18},{12,20},{14,22},{16,24},... | collective-permute-start | bytes 393224 | tf_op jit(solution)/shard_map/ppermute | solution.py:15
  33.4 4.3 %collective-permute-start.1 = (bf16[2,256,1,128]{1,3,2,0:T(8,128)(2,1)S(1)}, bf16[2,256,1,128]{1,3,2,0:T(8,128)(2,1)S(1)}, u32[]{:S(2)}, u32[]{:S(2)}) collective-permute-start(bf16[2,256,1,128]{1,3,2,0:T(8,128)(2,1)S(1)} %pad_maximum_fusion.1), channel_id=1, source_target_pairs={{0,6},{2,8},{4,10},{6,12},{8,14},{10,16},{12,18},{14,20},{16,22},{... | collective-permute-start | bytes 393224 | tf_op jit(solution)/shard_map/ppermute | solution.py:15
  37.7 3.4 %collective-permute-start.2 = (bf16[2,256,1,128]{1,3,2,0:T(8,128)(2,1)S(1)}, bf16[2,256,1,128]{1,3,2,0:T(8,128)(2,1)S(1)}, u32[]{:S(2)}, u32[]{:S(2)}) collective-permute-start(bf16[2,256,1,128]{1,3,2,0:T(8,128)(2,1)S(1)} %pad_maximum_fusion.1), channel_id=1, source_target_pairs={{0,4},{2,6},{4,8},{6,10},{8,12},{10,14},{12,16},{14,18},{16,20},{1... | collective-permute-start | bytes 393224 | tf_op jit(solution)/shard_map/ppermute | solution.py:15
  41.1 2.5 %collective-permute-start.3 = (bf16[2,256,1,128]{1,3,2,0:T(8,128)(2,1)S(1)}, bf16[2,256,1,128]{1,3,2,0:T(8,128)(2,1)S(1)}, u32[]{:S(2)}, u32[]{:S(2)}) collective-permute-start(bf16[2,256,1,128]{1,3,2,0:T(8,128)(2,1)S(1)} %pad_maximum_fusion.1), channel_id=1, source_target_pairs={{0,2},{2,4},{4,6},{6,8},{8,10},{10,12},{12,14},{14,16},{16,18},{18... | collective-permute-start | bytes 393224 | tf_op jit(solution)/shard_map/ppermute | solution.py:15
  43.6 0.6 multiply_reduce_fusion.1
  44.3 0.6 convolution_convert_fusion.1
  45.3 0.8 collective-permute-done.3
  46.2 0.8 fusion.60
  46.9 0.3 fusion.20
  47.2 0.3 fusion.17
  47.5 0.6 convolution_bitcast_fusion.1
  48.2 0.6 fusion.8
  48.8 0.6 convolution_bitcast_fusion.2
  49.3 1.1 %convolution_bitcast_fusion.3 = f32[256,2,128]{0,2,1:T(8,128)} fusion(bf16[2,256,1280]{1,2,0:T(8,128)(2,1)S(1)} %fusion.8, bf16[256,1,64]{0,2,1:T(8,128)(2,1)S(1)} %get-tuple-element.17, bf16[256,1,64]{0,2,1:T(8,128)(2,1)S(1)} %get-tuple-element.16, bf16[1024,1,128]{0,2,1:T(8,128)(2,1)S(1)} %get-tuple-element.9), kind=kOutput, calls=%fused_computation.28 | convolution fusion | flops 168755200 | bytes 1900544 | tf_op jit(solution)/shard_map/kgqc,ckh->qkgh/dot_general | solution.py:68
  50.6 0.8 fusion.59
  51.4 1.3 %collective-permute-start.4 = (bf16[2,256,1,128]{1,3,2,0:T(8,128)(2,1)}, bf16[2,256,1,128]{1,3,2,0:T(8,128)(2,1)}, u32[]{:S(2)}, u32[]{:S(2)}) collective-permute-start(bf16[2,256,1,128]{1,3,2,0:T(8,128)(2,1)} %get-tuple-element.4), channel_id=1, source_target_pairs={{2,0},{4,2},{6,4},{8,6},{10,8},{12,10},{14,12},{16,14},{18,16},{20... | collective-permute-start | bytes 393224 | tf_op jit(solution)/shard_map/ppermute | solution.py:15
  52.7 1.3 %collective-permute-start.5 = (bf16[2,256,1,128]{1,3,2,0:T(8,128)(2,1)}, bf16[2,256,1,128]{1,3,2,0:T(8,128)(2,1)}, u32[]{:S(2)}, u32[]{:S(2)}) collective-permute-start(bf16[2,256,1,128]{1,3,2,0:T(8,128)(2,1)} %get-tuple-element.7), channel_id=1, source_target_pairs={{4,0},{6,2},{8,4},{10,6},{12,8},{14,10},{16,12},{18,14},{20,16},{2... | collective-permute-start | bytes 393224 | tf_op jit(solution)/shard_map/ppermute | solution.py:15
  54.0 1.3 %collective-permute-start.6 = (bf16[2,256,1,128]{1,3,2,0:T(8,128)(2,1)}, bf16[2,256,1,128]{1,3,2,0:T(8,128)(2,1)}, u32[]{:S(2)}, u32[]{:S(2)}) collective-permute-start(bf16[2,256,1,128]{1,3,2,0:T(8,128)(2,1)} %get-tuple-element.6), channel_id=1, source_target_pairs={{6,0},{8,2},{10,4},{12,6},{14,8},{16,10},{18,12},{20,14},{22,16},{... | collective-permute-start | bytes 393224 | tf_op jit(solution)/shard_map/ppermute | solution.py:15
  55.3 1.3 %collective-permute-start.7 = (bf16[2,256,1,128]{1,3,2,0:T(8,128)(2,1)}, bf16[2,256,1,128]{1,3,2,0:T(8,128)(2,1)}, u32[]{:S(2)}, u32[]{:S(2)}) collective-permute-start(bf16[2,256,1,128]{1,3,2,0:T(8,128)(2,1)} %get-tuple-element.5), channel_id=1, source_target_pairs={{8,0},{10,2},{12,4},{14,6},{16,8},{18,10},{20,12},{22,14},{24,16},... | collective-permute-start | bytes 393224 | tf_op jit(solution)/shard_map/ppermute | solution.py:15
  56.6 1.7 %convolution_convert_fusion = bf16[256,2688]{1,0:T(8,128)(2,1)} fusion(bf16[256,256]{0,1:T(8,128)(2,1)S(1)} %bitcast.159, bf16[256,2688]{1,0:T(8,128)(2,1)S(1)} %copy-done), kind=kOutput, calls=%fused_computation.3 | convolution fusion | flops 353009664 | bytes 2883584 | tf_op jit(solution)/shard_map/dot_general | solution.py:164
  58.3 1.0 %multiply_add_fusion.1 = (f32[256,2,64]{0,2,1:T(8,128)S(1)}, f32[256,2,64]{0,2,1:T(8,128)S(1)}) fusion(f32[256,2,128]{0,2,1:T(8,128)} %convolution_bitcast_fusion.3, f32[256,64]{0,1:T(8,128)} %get-tuple-element.19, f32[256,64]{0,1:T(8,128)S(1)} %get-tuple-element.18), kind=kLoop, calls=%fused_computation.63 | loop fusion | flops 229376 | bytes 655360 | tf_op jit(solution)/shard_map/transpose(jvp())/add_any | solution.py:38
  59.4 1.1 %multiply_reduce_fusion = f32[256,2]{0,1:T(2,128)S(1)} fusion(f32[256,2,128]{0,2,1:T(8,128)} %copy-done.7, f32[256,2,64]{0,2,1:T(8,128)S(1)} %get-tuple-element.11, f32[256,2,64]{0,2,1:T(8,128)S(1)} %get-tuple-element.10, f32[128]{0:T(128)S(1)} %copy-done.16), kind=kLoop, calls=%fused_computation.46 | loop fusion | flops 261632 | bytes 526848 | tf_op jit(solution)/shard_map/transpose(jvp())/reduce_sum | solution.py:31
  60.4 1.1 %fusion.21 = bf16[256,2,128]{0,2,1:T(8,128)(2,1)S(1)} fusion(f32[256,2,128]{0,2,1:T(8,128)} %copy-done.7, f32[256,2,64]{0,2,1:T(8,128)S(1)} %get-tuple-element.11, f32[256,2,64]{0,2,1:T(8,128)S(1)} %get-tuple-element.10, f32[256,2]{0,1:T(2,128)S(1)} %multiply_multiply_fusion.1, f32[128]{0:T(128)S(1)} %copy-done.16, f32[256,2]{0,1:T(2,128)S(1)} %fusion.49), kind=kLoop, calls=%fused_computation.40 | loop fusion | flops 458752 | bytes 659968 | tf_op jit(solution)/shard_map/convert_element_type | solution.py:161
  61.5 0.6 fusion.61
  62.1 2.0 %collective-permute-done.5 = bf16[2,256,1,128]{1,3,2,0:T(8,128)(2,1)} collective-permute-done((bf16[2,256,1,128]{1,3,2,0:T(8,128)(2,1)}, bf16[2,256,1,128]{1,3,2,0:T(8,128)(2,1)}, u32[]{:S(2)}, u32[]{:S(2)}) %collective-permute-start.5) | collective-permute-done | bytes 131104 | tf_op jit(solution)/shard_map/ppermute | solution.py:15
  64.2 2.0 %collective-permute-done.6 = bf16[2,256,1,128]{1,3,2,0:T(8,128)(2,1)} collective-permute-done((bf16[2,256,1,128]{1,3,2,0:T(8,128)(2,1)}, bf16[2,256,1,128]{1,3,2,0:T(8,128)(2,1)}, u32[]{:S(2)}, u32[]{:S(2)}) %collective-permute-start.6) | collective-permute-done | bytes 131104 | tf_op jit(solution)/shard_map/ppermute | solution.py:15
  66.1 3.8 %collective-permute-done.7 = bf16[2,256,1,128]{1,3,2,0:T(8,128)(2,1)} collective-permute-done((bf16[2,256,1,128]{1,3,2,0:T(8,128)(2,1)}, bf16[2,256,1,128]{1,3,2,0:T(8,128)(2,1)}, u32[]{:S(2)}, u32[]{:S(2)}) %collective-permute-start.7) | collective-permute-done | bytes 131104 | tf_op jit(solution)/shard_map/ppermute | solution.py:15
  69.9 1.2 %convert_add_fusion = f32[2,256,1,128]{1,3,2,0:T(8,128)S(1)} fusion(bf16[2,256,1,128]{1,3,2,0:T(8,128)(2,1)} %collective-permute-done.7, bf16[2,256,1,128]{1,3,2,0:T(8,128)(2,1)} %collective-permute-done.6, bf16[2,256,1,128]{1,3,2,0:T(8,128)(2,1)} %collective-permute-done.5, bf16[2,256,1,128]{1,3,2,0:T(8,128)(2,1)} %collective-permute-done.4), kind=kLoop, calls=%fused_computation.45 | loop fusion | flops 458752 | bytes 786432 | tf_op jit(solution)/shard_map/add | solution.py:144
  71.1 0.9 fusion.26
  72.0 0.3 fusion.40
  72.5 0.6 convolution_add_fusion.1
  73.1 2.6 %fusion = bf16[256,2688]{1,0:T(8,128)(2,1)} fusion(f32[256,2688]{1,0:T(8,128)S(1)} %convolution_add_fusion.1, bf16[2688,128]{1,0:T(8,128)(2,1)S(1)} %copy-done.2, f32[2,256,1,128]{1,3,2,0:T(8,128)S(1)} %convert_add_fusion, f32[1280,1,128]{0,2,1:T(8,128)} %copy-done.10), kind=kOutput, calls=%fused_computation.2 | convolution fusion | flops 177602560 | bytes 5079040 | tf_op jit(solution)/shard_map/nh,dh->nd/dot_general | solution.py:172
  75.7 1.4 %reduce-scatter.3.cloned.1.call-done = bf16[128,2688]{1,0:T(8,128)(2,1)} async-done(((bf16[256,2688]{1,0:T(8,128)(2,1)}), bf16[128,2688]{1,0:T(8,128)(2,1)}) %reduce-scatter.3.cloned.1.call-update) | async-done | bytes 688144 | tf_op jit(solution)/shard_map/reduce_scatter | solution.py:176
  77.1 2.1 %add_convert_fusion.1 = bf16[128,2688]{1,0:T(8,128)(2,1)} fusion(bf16[128,2688]{1,0:T(8,128)(2,1)} %reduce-scatter.3.cloned.1.call-done, bf16[128,2688]{1,0:T(8,128)(2,1)S(1)} %copy-done.5), kind=kLoop, calls=%fused_computation.21 | loop fusion | flops 1376256 | bytes 2064384 | tf_op jit(solution)/shard_map/convert_element_type | solution.py:183
  79.2 10.2 %reduce-scatter.5.cloned.1.call-done = bf16[128,2688]{1,0:T(8,128)(2,1)} async-done(((bf16[256,2688]{1,0:T(8,128)(2,1)}), bf16[128,2688]{1,0:T(8,128)(2,1)}) %reduce-scatter.5.cloned.1.call-update) | async-done | bytes 688144 | tf_op jit(solution)/shard_map/reduce_scatter | solution.py:179
  89.5 2.1 %add_convert_fusion = bf16[128,2688]{1,0:T(8,128)(2,1)} fusion(bf16[128,2688]{1,0:T(8,128)(2,1)} %reduce-scatter.5.cloned.1.call-done, bf16[128,2688]{1,0:T(8,128)(2,1)S(1)} %copy-done.6), kind=kLoop, calls=%fused_computation.20 | loop fusion | flops 1376256 | bytes 2064384 | tf_op jit(solution)/shard_map/convert_element_type | solution.py:184
  (64 shorter events, 1.4 us)
Async XLA Ops:
  7.2 37.1 %copy-start = (bf16[256,2688]{1,0:T(8,128)(2,1)S(1)}, bf16[256,2688]{1,0:T(8,128)(2,1)}, u32[]{:S(2)}) copy-start(bf16[256,2688]{1,0:T(8,128)(2,1)} %param.13) | copy-start | bytes 4128772
  7.2 17.2 %all-gather.3.cloned.1.call-start = ((), (), s32[]{:S(2)}) async-start(), calls=%async_computation.4 | async-start | bytes 4128768 | tf_op jit(solution)/shard_map/all_gather | solution.py:89
  9.9 1.3 %copy-start.1 = (bf16[2688,256]{1,0:T(8,128)(2,1)S(1)}, bf16[2688,256]{1,0:T(8,128)(2,1)}, u32[]{:S(2)}) copy-start(bf16[2688,256]{1,0:T(8,128)(2,1)} %param.10) | copy-start | bytes 4128772
  9.9 67.2 %reduce-scatter.3.cloned.1.call-start = ((), (), s32[]{:S(2)}) async-start(), calls=%async_computation.2 | async-start | bytes 2064384 | tf_op jit(solution)/shard_map/reduce_scatter | solution.py:176
  26.3 1.1 %copy-start.3 = (bf16[2688,128]{1,0:T(8,128)(2,1)S(1)}, bf16[2688,128]{1,0:T(8,128)(2,1)}, u32[]{:S(2)}) copy-start(bf16[2688,128]{1,0:T(8,128)(2,1)} %param.11) | copy-start | bytes 2064388
  26.6 2.1 %copy-start.15 = (f32[128]{0:T(128)S(1)}, f32[128]{0:T(128)}, u32[]{:S(2)}) copy-start(f32[128]{0:T(128)} %param.15) | copy-start | bytes 1540
  26.6 2.6 %copy-start.2 = (bf16[2688,128]{1,0:T(8,128)(2,1)S(1)}, bf16[2688,128]{1,0:T(8,128)(2,1)}, u32[]{:S(2)}) copy-start(bf16[2688,128]{1,0:T(8,128)(2,1)} %param.12) | copy-start | bytes 2064388
  28.1 0.7 copy-start.8
  28.7 14.9 %copy-start.12 = (bf16[256,2688]{1,0:T(8,128)(2,1)S(1)}, bf16[256,2688]{1,0:T(8,128)(2,1)}, u32[]{:S(2)}) copy-start(bf16[256,2688]{1,0:T(8,128)(2,1)} %copy.42) | copy-start | bytes 4128772
  29.8 15.5 %collective-permute-start = (bf16[2,256,1,128]{1,3,2,0:T(8,128)(2,1)S(1)}, bf16[2,256,1,128]{1,3,2,0:T(8,128)(2,1)S(1)}, u32[]{:S(2)}, u32[]{:S(2)}) collective-permute-start(bf16[2,256,1,128]{1,3,2,0:T(8,128)(2,1)S(1)} %pad_maximum_fusion.1), channel_id=1, source_target_pairs={{0,8},{2,10},{4,12},{6,14},{8,16},{10,18},{12,20},{14,22},{16,24},... | collective-permute-start | bytes 393224 | tf_op jit(solution)/shard_map/ppermute | solution.py:15
  33.4 11.8 %collective-permute-start.1 = (bf16[2,256,1,128]{1,3,2,0:T(8,128)(2,1)S(1)}, bf16[2,256,1,128]{1,3,2,0:T(8,128)(2,1)S(1)}, u32[]{:S(2)}, u32[]{:S(2)}) collective-permute-start(bf16[2,256,1,128]{1,3,2,0:T(8,128)(2,1)S(1)} %pad_maximum_fusion.1), channel_id=1, source_target_pairs={{0,6},{2,8},{4,10},{6,12},{8,14},{10,16},{12,18},{14,20},{16,22},{... | collective-permute-start | bytes 393224 | tf_op jit(solution)/shard_map/ppermute | solution.py:15
  37.7 7.5 %collective-permute-start.2 = (bf16[2,256,1,128]{1,3,2,0:T(8,128)(2,1)S(1)}, bf16[2,256,1,128]{1,3,2,0:T(8,128)(2,1)S(1)}, u32[]{:S(2)}, u32[]{:S(2)}) collective-permute-start(bf16[2,256,1,128]{1,3,2,0:T(8,128)(2,1)S(1)} %pad_maximum_fusion.1), channel_id=1, source_target_pairs={{0,4},{2,6},{4,8},{6,10},{8,12},{10,14},{12,16},{14,18},{16,20},{1... | collective-permute-start | bytes 393224 | tf_op jit(solution)/shard_map/ppermute | solution.py:15
  41.1 5.0 %collective-permute-start.3 = (bf16[2,256,1,128]{1,3,2,0:T(8,128)(2,1)S(1)}, bf16[2,256,1,128]{1,3,2,0:T(8,128)(2,1)S(1)}, u32[]{:S(2)}, u32[]{:S(2)}) collective-permute-start(bf16[2,256,1,128]{1,3,2,0:T(8,128)(2,1)S(1)} %pad_maximum_fusion.1), channel_id=1, source_target_pairs={{0,2},{2,4},{4,6},{6,8},{8,10},{10,12},{12,14},{14,16},{16,18},{18... | collective-permute-start | bytes 393224 | tf_op jit(solution)/shard_map/ppermute | solution.py:15
  44.2 0.7 copy-start.7
  44.2 0.7 copy-start.16
  44.3 0.9 copy-start.13
  45.0 1.1 %copy-start.14 = (pred[256,1280]{0,1:T(8,128)(4,1)S(1)}, pred[256,1280]{0,1:T(8,128)(4,1)}, u32[]{:S(2)}) copy-start(pred[256,1280]{0,1:T(8,128)(4,1)} %fusion.13) | copy-start | bytes 983044
  48.1 2.3 %copy-start.10 = (f32[1280,1,128]{0,2,1:T(8,128)}, f32[1280,1,128]{0,2,1:T(8,128)S(1)}, u32[]{:S(2)}) copy-start(f32[1280,1,128]{0,2,1:T(8,128)S(1)} %convolution_bitcast_fusion.1) | copy-start | bytes 1966084
  49.3 1.2 %copy-start.11 = (f32[1280,1,128]{0,2,1:T(8,128)}, f32[1280,1,128]{0,2,1:T(8,128)S(1)}, u32[]{:S(2)}) copy-start(f32[1280,1,128]{0,2,1:T(8,128)S(1)} %convolution_bitcast_fusion.2) | copy-start | bytes 1966084
  51.4 10.7 %collective-permute-start.4 = (bf16[2,256,1,128]{1,3,2,0:T(8,128)(2,1)}, bf16[2,256,1,128]{1,3,2,0:T(8,128)(2,1)}, u32[]{:S(2)}, u32[]{:S(2)}) collective-permute-start(bf16[2,256,1,128]{1,3,2,0:T(8,128)(2,1)} %get-tuple-element.4), channel_id=1, source_target_pairs={{2,0},{4,2},{6,4},{8,6},{10,8},{12,10},{14,12},{16,14},{18,16},{20... | collective-permute-start | bytes 393224 | tf_op jit(solution)/shard_map/ppermute | solution.py:15
  52.7 11.5 %collective-permute-start.5 = (bf16[2,256,1,128]{1,3,2,0:T(8,128)(2,1)}, bf16[2,256,1,128]{1,3,2,0:T(8,128)(2,1)}, u32[]{:S(2)}, u32[]{:S(2)}) collective-permute-start(bf16[2,256,1,128]{1,3,2,0:T(8,128)(2,1)} %get-tuple-element.7), channel_id=1, source_target_pairs={{4,0},{6,2},{8,4},{10,6},{12,8},{14,10},{16,12},{18,14},{20,16},{2... | collective-permute-start | bytes 393224 | tf_op jit(solution)/shard_map/ppermute | solution.py:15
  54.0 12.1 %collective-permute-start.6 = (bf16[2,256,1,128]{1,3,2,0:T(8,128)(2,1)}, bf16[2,256,1,128]{1,3,2,0:T(8,128)(2,1)}, u32[]{:S(2)}, u32[]{:S(2)}) collective-permute-start(bf16[2,256,1,128]{1,3,2,0:T(8,128)(2,1)} %get-tuple-element.6), channel_id=1, source_target_pairs={{6,0},{8,2},{10,4},{12,6},{14,8},{16,10},{18,12},{20,14},{22,16},{... | collective-permute-start | bytes 393224 | tf_op jit(solution)/shard_map/ppermute | solution.py:15
  55.3 14.7 %collective-permute-start.7 = (bf16[2,256,1,128]{1,3,2,0:T(8,128)(2,1)}, bf16[2,256,1,128]{1,3,2,0:T(8,128)(2,1)}, u32[]{:S(2)}, u32[]{:S(2)}) collective-permute-start(bf16[2,256,1,128]{1,3,2,0:T(8,128)(2,1)} %get-tuple-element.5), channel_id=1, source_target_pairs={{8,0},{10,2},{12,4},{14,6},{16,8},{18,10},{20,12},{22,14},{24,16},... | collective-permute-start | bytes 393224 | tf_op jit(solution)/shard_map/ppermute | solution.py:15
  58.3 31.2 %reduce-scatter.5.cloned.1.call-start = ((), (), s32[]{:S(2)}) async-start(), calls=%async_computation.3 | async-start | bytes 2064384 | tf_op jit(solution)/shard_map/reduce_scatter | solution.py:179
  62.1 10.3 %copy-start.9 = (f32[256,128]{0,1:T(8,128)S(1)}, f32[256,128]{0,1:T(8,128)}, u32[]{:S(2)}) copy-start(f32[256,128]{0,1:T(8,128)} %copy-done.8) | copy-start | bytes 393220
  62.1 10.4 %copy-start.4 = (bf16[2688,128]{1,0:T(8,128)(2,1)S(1)}, bf16[2688,128]{1,0:T(8,128)(2,1)}, u32[]{:S(2)}) copy-start(bf16[2688,128]{1,0:T(8,128)(2,1)} %param.11) | copy-start | bytes 2064388
  75.7 1.4 %copy-start.5 = (bf16[128,2688]{1,0:T(8,128)(2,1)S(1)}, bf16[128,2688]{1,0:T(8,128)(2,1)}, u32[]{:S(2)}) copy-start(bf16[128,2688]{1,0:T(8,128)(2,1)} %param.8) | copy-start | bytes 2064388
  75.7 13.7 %copy-start.6 = (bf16[128,2688]{1,0:T(8,128)(2,1)S(1)}, bf16[128,2688]{1,0:T(8,128)(2,1)}, u32[]{:S(2)}) copy-start(bf16[128,2688]{1,0:T(8,128)(2,1)} %param.9) | copy-start | bytes 2064388
Sparse Core Ops, SparseCore 0:
  10.0 14.2 all-gather.2
  58.4 18.6 reduce-scatter.2
  79.4 10.0 reduce-scatter.4
